TPU v7x, 256 devices: a whole 4x4x8 slice. The times are simulated.
256 devices in a mesh: ctx: 16 (over z_hi, y, core), exp: 16 (over z_lo, x).
Axes of the slice: x: 4, y: 4, z: 8 (z_hi: 2, z_lo: 4; z = z_hi * 4 + z_lo), core: 2. Of those that a mesh axis runs over, the one named last changes fastest.
Arguments:
- residual: bfloat16 [16, 2048, 7168], P('exp', 'ctx'), may hold values from -6 to 6
- queries: bfloat16 [16, 2048, 1024], P('exp', 'ctx'), may hold values from -64 to 64
- latent: bfloat16 [16, 2048, 512], P('exp', 'ctx'), may hold values from -6 to 6
- out_proj: bfloat16 [1024, 7168], P('ctx'), may hold values from -0.5 to 0.5
- up_weight: bfloat16 [16, 7168, 1024], P('exp', 'ctx'), may hold values from -0.0625 to 0.0625
- down_weight: bfloat16 [16, 1024, 7168], P('exp', None, 'ctx'), may hold values from -0.1875 to 0.1875
- cotangent: bfloat16 [16, 2048, 7168], P('exp', 'ctx'), may hold values from -6 to 6
- routes: int32 [16, 2048, 8], P('exp', 'ctx'), may hold values from 0 to 255, as said below
- gate_values: float32 [16, 2048, 8], P('exp', 'ctx'), may hold values from 0.2 to 1
- documents: int32 [16, 16], P('exp'), may hold values from 0 to 2, never falling along the last dimension, each value on 1 to 8 neighbouring positions
Outputs:
- layer_out: bfloat16 [16, 2048, 7168], P('exp', 'ctx')
- input_grad: bfloat16 [16, 2048, 7168], P('exp', 'ctx')
- up_grad: bfloat16 [16, 7168, 1024], P('exp', 'ctx')
- down_grad: bfloat16 [16, 1024, 7168], P('exp', None, 'ctx')
Inputs may be any that keep to these rules, and one draw needn't show every extreme that they name: Each token's 8 experts differ. Within one block of 128 consecutive tokens of a sequence at most 4 routes name one expert below 16, and in every draw some expert below 16 is named by exactly 4 routes of every such block. `documents`: document numbers never fall along a sequence; a document covers 1 to 8 consecutive blocks, and one covers exactly 8.
All inputs are finite; a program needn't handle non-finite values.
Results may differ from a plain program's by a relative error of at most 0.025.
Values may be sent and summed in bfloat16 or wider, within the bound.
No kernel may reach another device: no remote copies, remote signals or barrier semaphores. Data moves between devices by JAX's collectives and lax.ppermute only.
A program may use at most 128 MiB of HBM per device.

v0:
```python
import math
import jax
import jax.numpy as jnp
from jax import lax
from jax.sharding import PartitionSpec as P

LAT = 512
HEADS = 2
CAP = 4
BLOCK = 128


def shifted(shard, axis, by):
    peers = lax.axis_size(axis)
    pairs = [(i, i + by) for i in range(peers) if 0 <= i + by < peers]
    return lax.ppermute(shard, axis, pairs)


def split_up(shard, dim, peers):
    dims = shard.shape
    pieces = shard.reshape(*dims[:dim], peers, dims[dim] // peers, *dims[dim + 1 :])
    return jnp.moveaxis(pieces, dim, 0)


def laid_out(pieces, dim):
    pieces = jnp.moveaxis(pieces, 0, dim)
    dims = pieces.shape
    return pieces.reshape(*dims[:dim], dims[dim] * dims[dim + 1], *dims[dim + 2 :])


def joined_exchange(shard, axis, axes, splits, concats):
    sizes = [lax.axis_size(a) for a in axes]
    pieces = split_up(shard, splits[0], sizes[0])
    pieces = jnp.moveaxis(split_up(pieces, splits[1] + 1, sizes[1]), 0, 1)
    inside = pieces.shape[2:]
    pieces = pieces.reshape(-1, *inside)
    pieces = lax.all_to_all(pieces, axis, split_axis=0, concat_axis=0, tiled=True)
    pieces = laid_out(pieces.reshape(*sizes, *inside), concats[0] + 1)
    return laid_out(pieces, concats[1])


def silu_grad(values_in):
    sigmoid_of = jax.nn.sigmoid(values_in)
    return sigmoid_of * (1.0 + values_in * (1.0 - sigmoid_of))


def slot_tables(route_rows, gate_rows, expert_total, capacity):
    experts = jnp.arange(expert_total, dtype=jnp.int32)
    onehot = (route_rows[:, :, None] == experts[None, None, :]).astype(jnp.int32)
    flat_hits = onehot.reshape(-1, expert_total)
    before = jnp.cumsum(flat_hits, axis=0) - flat_hits
    rank_in = jnp.sum(before * flat_hits, axis=1).reshape(route_rows.shape)
    valid = route_rows < expert_total
    slot_index = jnp.where(valid, route_rows * capacity + rank_in, -1)
    slots_all = jnp.arange(expert_total * capacity, dtype=jnp.int32)
    slot_hits = slot_index[None, :, :] == slots_all[:, None, None]
    picker = jnp.sum(slot_hits.astype(jnp.float32), axis=2)
    weigher = jnp.sum(jnp.where(slot_hits, gate_rows[None, :, :], 0.0), axis=2)
    return (picker, weigher)


def shards(
    residual,
    queries,
    latent,
    out_proj,
    up_weight,
    down_weight,
    cotangent,
    routes,
    gate_values,
    documents,
):
    ctx_count = lax.axis_size("ctx")
    exp_count = lax.axis_size("exp")
    my_index = lax.axis_index("ctx")
    tokens = residual.shape[1]
    model_width = residual.shape[2]
    doc_row = documents[0]
    block_total = doc_row.shape[0]
    inv_root = 1.0 / math.sqrt(LAT)
    query_rows = queries[0].reshape(tokens, HEADS, LAT)
    token_iota = jnp.arange(tokens, dtype=jnp.int32)
    block_iota = jnp.arange(block_total, dtype=jnp.int32)

    def doc_of(positions):
        matches = (positions // BLOCK)[:, None] == block_iota[None, :]
        return jnp.sum(jnp.where(matches, doc_row[None, :], 0), axis=1)

    query_pos = my_index * tokens + token_iota
    query_doc = doc_of(query_pos)

    def fold_keys(running_max, running_sum, weighted, key_block, source):
        key_pos = source * tokens + token_iota
        allowed = (
            (query_doc[:, None] == doc_of(key_pos)[None, :])
            & (key_pos[None, :] <= query_pos[:, None])
            & (source >= 0)
        )
        scores = (
            jnp.einsum("thk,jk->thj", query_rows, key_block, preferred_element_type=jnp.float32)
            * inv_root
        )
        scores = jnp.where(allowed[:, None, :], scores, -1e30)
        new_max = jnp.maximum(running_max, jnp.max(scores, axis=2))
        exponent = jnp.where(allowed[:, None, :], jnp.exp(scores - new_max[:, :, None]), 0.0)
        rescale = jnp.exp(running_max - new_max)
        running_sum = running_sum * rescale + jnp.sum(exponent, axis=2)
        weighted = weighted * rescale[:, :, None] + jnp.einsum(
            "thj,jk->thk",
            exponent.astype(jnp.bfloat16),
            key_block,
            preferred_element_type=jnp.float32,
        )
        return (new_max, running_sum, weighted)

    start_max = jnp.full((tokens, HEADS), -1e30, jnp.float32)
    start_sum = jnp.zeros((tokens, HEADS), jnp.float32)
    start_acc = jnp.zeros((tokens, HEADS, LAT), jnp.float32)
    first_max, first_sum, first_acc = fold_keys(
        start_max, start_sum, start_acc, latent[0], my_index
    )
    cycle_turns = ctx_count - 1

    def cycle_turn(cycle_step, loop_carry):
        key_block, running_max, running_sum, weighted = loop_carry
        key_block = shifted(key_block, "ctx", 1)
        running_max, running_sum, weighted = fold_keys(
            running_max, running_sum, weighted, key_block, my_index - cycle_step
        )
        return (key_block, running_max, running_sum, weighted)

    loop_carry = lax.fori_loop(
        1, cycle_turns + 1, cycle_turn, (latent[0], first_max, first_sum, first_acc)
    )
    heads_out = (
        (loop_carry[3] / loop_carry[2][:, :, None])
        .astype(jnp.bfloat16)
        .reshape(tokens, HEADS * LAT)
    )
    projected = jnp.dot(
        heads_out,
        lax.all_gather(out_proj, "ctx", axis=0, tiled=True),
        preferred_element_type=jnp.float32,
    )
    hidden_in = (residual[0].astype(jnp.float32) + projected).astype(jnp.bfloat16)
    picker, weigher = slot_tables(routes[0], gate_values[0], exp_count, CAP)
    picker_half = picker.astype(jnp.bfloat16)
    slot_gate = jnp.sum(weigher, axis=1)
    slot_in = jnp.dot(picker_half, hidden_in, preferred_element_type=jnp.float32).astype(
        jnp.bfloat16
    )
    slot_cot = (
        jnp.dot(picker_half, cotangent[0], preferred_element_type=jnp.float32) * slot_gate[:, None]
    ).astype(jnp.bfloat16)
    slot_in = slot_in.reshape(1, exp_count, CAP, model_width)
    slot_cot = slot_cot.reshape(1, exp_count, CAP, model_width)
    arrived_in, arrived_cot = (
        joined_exchange(slot_in, ("ctx", "exp"), ("ctx", "exp"), (3, 1), (0, 1)),
        joined_exchange(slot_cot, ("ctx", "exp"), ("ctx", "exp"), (3, 1), (0, 1)),
    )
    part_width = model_width // ctx_count
    row_total = ctx_count * exp_count * CAP
    in_rows = arrived_in.reshape(row_total, part_width)
    cot_rows = arrived_cot.reshape(row_total, part_width)
    up_part = up_weight[0]
    down_part = down_weight[0]
    contract_rows = (((0,), (0,)), ((), ()))
    contract_cols = (((1,), (1,)), ((), ()))

    def sum_all(term_rows):
        return lax.psum(term_rows.astype(jnp.bfloat16), "ctx").astype(jnp.float32)

    pre_full = sum_all(jnp.dot(in_rows, up_part, preferred_element_type=jnp.float32))
    activated = jax.nn.silu(pre_full).astype(jnp.bfloat16)
    grad_full = sum_all(
        lax.dot_general(cot_rows, down_part, contract_cols, preferred_element_type=jnp.float32)
    )
    pre_grad = (grad_full * silu_grad(pre_full)).astype(jnp.bfloat16)
    slot_out = jnp.dot(activated, down_part, preferred_element_type=jnp.float32).astype(
        jnp.bfloat16
    )
    down_grad = lax.dot_general(
        activated, cot_rows, contract_rows, preferred_element_type=jnp.float32
    ).astype(jnp.bfloat16)
    up_grad = lax.dot_general(
        in_rows, pre_grad, contract_rows, preferred_element_type=jnp.float32
    ).astype(jnp.bfloat16)
    slot_in_grad = lax.dot_general(
        pre_grad, up_part, contract_cols, preferred_element_type=jnp.float32
    ).astype(jnp.bfloat16)
    returned_out, returned_grad = (
        joined_exchange(
            slot_out.reshape(ctx_count, exp_count, CAP, part_width),
            ("ctx", "exp"),
            ("ctx", "exp"),
            (0, 1),
            (3, 1),
        ),
        joined_exchange(
            slot_in_grad.reshape(ctx_count, exp_count, CAP, part_width),
            ("ctx", "exp"),
            ("ctx", "exp"),
            (0, 1),
            (3, 1),
        ),
    )
    flat_out = returned_out.reshape(exp_count * CAP, model_width).astype(jnp.float32)
    flat_grad = returned_grad.reshape(exp_count * CAP, model_width).astype(jnp.float32)
    gathered_out = lax.dot_general(
        weigher,
        flat_out,
        contract_rows,
        precision=lax.Precision.HIGHEST,
        preferred_element_type=jnp.float32,
    )
    gathered_grad = lax.dot_general(
        picker,
        flat_grad,
        contract_rows,
        precision=lax.Precision.HIGHEST,
        preferred_element_type=jnp.float32,
    )
    layer_out = (hidden_in.astype(jnp.float32) + gathered_out).astype(jnp.bfloat16)
    input_grad = (cotangent[0].astype(jnp.float32) + gathered_grad).astype(jnp.bfloat16)
    return (layer_out[None], input_grad[None], up_grad[None], down_grad[None])


def solution(mesh):
    placed = (
        P("exp", "ctx", None),
        P("exp", "ctx", None),
        P("exp", "ctx", None),
        P("ctx", None),
        P("exp", "ctx", None),
        P("exp", None, "ctx"),
        P("exp", "ctx", None),
        P("exp", "ctx", None),
        P("exp", "ctx", None),
        P("exp", None),
    )
    return jax.shard_map(
        shards,
        mesh=mesh,
        in_specs=placed,
        out_specs=(
            P("exp", "ctx", None),
            P("exp", "ctx", None),
            P("exp", "ctx", None),
            P("exp", None, "ctx"),
        ),
        check_vma=False,
    )
```

profile of v0, /device:TPU:1, one launch (start us, length us, event | category | flops | bytes accessed | tf_op | source)
XLA Modules:
  0.0 664.1 jit_solution(6608124247840334252)
XLA Ops:
  9.3 4.5 reduce-window.6
  16.4 2.3 reshape_reshape.14
  21.1 16.7 %all-to-all-start.2 = ((bf16[256,1,1,4,448]{4,3,2,1,0:T(4,128)(2,1)}), bf16[256,1,1,4,448]{4,3,2,1,0:T(4,128)(2,1)}, u32[]{:S(2)}, u32[]{:S(2)}) async-start(bf16[256,1,1,4,448]{4,3,2,1,0:T(4,128)(2,1)} %copy.110), calls=%async_computation.2 | async-start | bytes 2097152 | tf_op jit(solution)/shard_map/all_to_all | solution.py:37
  38.9 201.2 %while.22 = (s32[]{:T(128)}, bf16[128,512]{1,0:T(8,128)(2,1)S(1)}, f32[128,2]{0,1:T(2,128)S(1)}, f32[128,2]{0,1:T(2,128)S(1)}, f32[128,2,512]{2,0,1:T(8,128)S(1)...) while((s32[]{:T(128)}, bf16[128,512]{1,0:T(8,128)(2,1)S(1)}, ...), condition=%wide.region_7.8_spmd.clone, body=%wide.region_3.7_spmd.clone.sunk | while | flops 67740288 | bytes 2839315 | solution.py:133
  38.9 3.5 collective-permute-start
  42.7 2.6 collective-permute-done
  46.0 4.4 collective-permute-start
  50.6 2.6 collective-permute-done
  53.9 4.4 collective-permute-start
  58.6 4.3 collective-permute-done
  63.6 5.2 collective-permute-start
  69.0 2.9 collective-permute-done
  72.5 4.4 collective-permute-start
  79.6 4.4 collective-permute-start
  86.6 13.3 %collective-permute-start = (bf16[128,512]{1,0:T(8,128)(2,1)S(1)}, bf16[128,512]{1,0:T(8,128)(2,1)S(1)}, u32[]{:S(2)}, u32[]{:S(2)}) collective-permute-start(bf16[128,512]{1,0:T(8,128)(2,1)S(1)} %get-tuple-element.483), channel_id=1, source_target_pairs={{0,16},{16,32},{32,48},{48,64},{64,80},{80,96},{96,112},{112,128},... | collective-permute-start | bytes 393224 | tf_op jit(solution)/shard_map/while/body/eval_jaxpr/ppermute | solution.py:16
  102.5 10.9 %collective-permute-start = (bf16[128,512]{1,0:T(8,128)(2,1)S(1)}, bf16[128,512]{1,0:T(8,128)(2,1)S(1)}, u32[]{:S(2)}, u32[]{:S(2)}) collective-permute-start(bf16[128,512]{1,0:T(8,128)(2,1)S(1)} %get-tuple-element.483), channel_id=1, source_target_pairs={{0,16},{16,32},{32,48},{48,64},{64,80},{80,96},{96,112},{112,128},... | collective-permute-start | bytes 393224 | tf_op jit(solution)/shard_map/while/body/eval_jaxpr/ppermute | solution.py:16
  116.1 12.3 %collective-permute-start = (bf16[128,512]{1,0:T(8,128)(2,1)S(1)}, bf16[128,512]{1,0:T(8,128)(2,1)S(1)}, u32[]{:S(2)}, u32[]{:S(2)}) collective-permute-start(bf16[128,512]{1,0:T(8,128)(2,1)S(1)} %get-tuple-element.483), channel_id=1, source_target_pairs={{0,16},{16,32},{32,48},{48,64},{64,80},{80,96},{96,112},{112,128},... | collective-permute-start | bytes 393224 | tf_op jit(solution)/shard_map/while/body/eval_jaxpr/ppermute | solution.py:16
  131.4 16.8 %collective-permute-start = (bf16[128,512]{1,0:T(8,128)(2,1)S(1)}, bf16[128,512]{1,0:T(8,128)(2,1)S(1)}, u32[]{:S(2)}, u32[]{:S(2)}) collective-permute-start(bf16[128,512]{1,0:T(8,128)(2,1)S(1)} %get-tuple-element.483), channel_id=1, source_target_pairs={{0,16},{16,32},{32,48},{48,64},{64,80},{80,96},{96,112},{112,128},... | collective-permute-start | bytes 393224 | tf_op jit(solution)/shard_map/while/body/eval_jaxpr/ppermute | solution.py:16
  150.8 18.1 %collective-permute-start = (bf16[128,512]{1,0:T(8,128)(2,1)S(1)}, bf16[128,512]{1,0:T(8,128)(2,1)S(1)}, u32[]{:S(2)}, u32[]{:S(2)}) collective-permute-start(bf16[128,512]{1,0:T(8,128)(2,1)S(1)} %get-tuple-element.483), channel_id=1, source_target_pairs={{0,16},{16,32},{32,48},{48,64},{64,80},{80,96},{96,112},{112,128},... | collective-permute-start | bytes 393224 | tf_op jit(solution)/shard_map/while/body/eval_jaxpr/ppermute | solution.py:16
  171.6 29.1 %collective-permute-start = (bf16[128,512]{1,0:T(8,128)(2,1)S(1)}, bf16[128,512]{1,0:T(8,128)(2,1)S(1)}, u32[]{:S(2)}, u32[]{:S(2)}) collective-permute-start(bf16[128,512]{1,0:T(8,128)(2,1)S(1)} %get-tuple-element.483), channel_id=1, source_target_pairs={{0,16},{16,32},{32,48},{48,64},{64,80},{80,96},{96,112},{112,128},... | collective-permute-start | bytes 393224 | tf_op jit(solution)/shard_map/while/body/eval_jaxpr/ppermute | solution.py:16
  203.3 8.0 %collective-permute-start = (bf16[128,512]{1,0:T(8,128)(2,1)S(1)}, bf16[128,512]{1,0:T(8,128)(2,1)S(1)}, u32[]{:S(2)}, u32[]{:S(2)}) collective-permute-start(bf16[128,512]{1,0:T(8,128)(2,1)S(1)} %get-tuple-element.483), channel_id=1, source_target_pairs={{0,16},{16,32},{32,48},{48,64},{64,80},{80,96},{96,112},{112,128},... | collective-permute-start | bytes 393224 | tf_op jit(solution)/shard_map/while/body/eval_jaxpr/ppermute | solution.py:16
  214.0 10.5 %collective-permute-start = (bf16[128,512]{1,0:T(8,128)(2,1)S(1)}, bf16[128,512]{1,0:T(8,128)(2,1)S(1)}, u32[]{:S(2)}, u32[]{:S(2)}) collective-permute-start(bf16[128,512]{1,0:T(8,128)(2,1)S(1)} %get-tuple-element.483), channel_id=1, source_target_pairs={{0,16},{16,32},{32,48},{48,64},{64,80},{80,96},{96,112},{112,128},... | collective-permute-start | bytes 393224 | tf_op jit(solution)/shard_map/while/body/eval_jaxpr/ppermute | solution.py:16
  227.1 10.4 %collective-permute-start = (bf16[128,512]{1,0:T(8,128)(2,1)S(1)}, bf16[128,512]{1,0:T(8,128)(2,1)S(1)}, u32[]{:S(2)}, u32[]{:S(2)}) collective-permute-start(bf16[128,512]{1,0:T(8,128)(2,1)S(1)} %get-tuple-element.483), channel_id=1, source_target_pairs={{0,16},{16,32},{32,48},{48,64},{64,80},{80,96},{96,112},{112,128},... | collective-permute-start | bytes 393224 | tf_op jit(solution)/shard_map/while/body/eval_jaxpr/ppermute | solution.py:16
  240.4 8.3 %fusion.16 = bf16[128,7168]{1,0:T(8,128)(2,1)S(1)} fusion(bf16[128,1024]{0,1:T(8,128)(2,1)S(1)} %bitcast.139, bf16[1024,7168]{1,0:T(8,128)(2,1)} %all-gather.2.cloned.1.call-done, bf16[1,128,7168]{2,1,0:T(8,128)(2,1)} %param.12), kind=kOutput, calls=%fused_computation.29 | convolution fusion | flops 1881800704 | bytes 18612224 | tf_op jit(solution)/shard_map/dot_general | solution.py:141
  249.9 3.1 reshape_reshape.12
  256.6 69.9 %all-to-all-start = ((bf16[256,1,1,4,448]{4,3,2,1,0:T(4,128)(2,1)}), bf16[256,1,1,4,448]{4,3,2,1,0:T(4,128)(2,1)}, u32[]{:S(2)}, u32[]{:S(2)}) async-start(bf16[256,1,1,4,448]{4,3,2,1,0:T(4,128)(2,1)} %copy.105), calls=%async_computation | async-start | bytes 2097152 | tf_op jit(solution)/shard_map/all_to_all | solution.py:37
  326.8 2.4 reshape_reshape.15
  329.2 4.0 convolution_convert_fusion.1
  333.3 24.4 %all-to-all-done = bf16[256,1,1,4,448]{4,3,2,1,0:T(4,128)(2,1)} async-done(((bf16[256,1,1,4,448]{4,3,2,1,0:T(4,128)(2,1)}), bf16[256,1,1,4,448]{4,3,2,1,0:T(4,128)(2,1)}, u32[]{:S(2)}, u32[]{:S(2)}) %all-to-all-start) | async-done | bytes 917536 | tf_op jit(solution)/shard_map/all_to_all | solution.py:37
  357.7 2.4 reshape_reshape.13
  360.1 3.8 convolution_convert_fusion.2
  363.9 187.7 %all-reduce.3.cloned.1.call-done = (bf16[1024,1024]{1,0:T(8,128)(2,1)}, bf16[1024,1024]{1,0:T(8,128)(2,1)}) async-done(((bf16[1024,1024]{1,0:T(8,128)(2,1)}, bf16[1024,1024]{1,0:T(8,128)(2,1)}), (bf16[1024,1024]{1,0:T(8,128)(2,1)}, bf16[1024,1024]{1,0:T(8,128)(2,1)})) %all-reduce.3.cloned.1.call-update) | async-done | bytes 4194320 | tf_op jit(solution)/shard_map/psum | solution.py:172
  551.6 3.9 fusion.29
  558.9 2.3 copy.111
  563.3 14.0 %all-to-all-start.3 = ((bf16[256,1,1,4,448]{4,3,2,1,0:T(4,128)(2,1)}), bf16[256,1,1,4,448]{4,3,2,1,0:T(4,128)(2,1)}, u32[]{:S(2)}, u32[]{:S(2)}) async-start(bf16[256,1,1,4,448]{4,3,2,1,0:T(4,128)(2,1)} %bitcast.131), calls=%async_computation.3 | async-start | bytes 2097152 | tf_op jit(solution)/shard_map/all_to_all | solution.py:37
  577.3 4.3 convolution_convert_fusion.6
  581.6 2.3 copy.106
  586.0 22.4 %all-to-all-done.3 = bf16[256,1,1,4,448]{4,3,2,1,0:T(4,128)(2,1)} async-done(((bf16[256,1,1,4,448]{4,3,2,1,0:T(4,128)(2,1)}), bf16[256,1,1,4,448]{4,3,2,1,0:T(4,128)(2,1)}, u32[]{:S(2)}, u32[]{:S(2)}) %all-to-all-start.3) | async-done | bytes 917536 | tf_op jit(solution)/shard_map/all_to_all | solution.py:37
  608.4 7.7 %all-to-all-start.1 = ((bf16[256,1,1,4,448]{4,3,2,1,0:T(4,128)(2,1)}), bf16[256,1,1,4,448]{4,3,2,1,0:T(4,128)(2,1)}, u32[]{:S(2)}, u32[]{:S(2)}) async-start(bf16[256,1,1,4,448]{4,3,2,1,0:T(4,128)(2,1)} %bitcast.130), calls=%async_computation.1 | async-start | bytes 2097152 | tf_op jit(solution)/shard_map/all_to_all | solution.py:37
  616.2 4.1 fusion.31
  620.3 2.5 fusion.32
  622.8 2.8 copy.121
  625.6 2.9 reshape_reshape_transpose_reshape.7
  628.5 4.7 fusion.19
  633.3 14.2 %all-to-all-done.1 = bf16[256,1,1,4,448]{4,3,2,1,0:T(4,128)(2,1)} async-done(((bf16[256,1,1,4,448]{4,3,2,1,0:T(4,128)(2,1)}), bf16[256,1,1,4,448]{4,3,2,1,0:T(4,128)(2,1)}, u32[]{:S(2)}, u32[]{:S(2)}) %all-to-all-start.1) | async-done | bytes 917536 | tf_op jit(solution)/shard_map/all_to_all | solution.py:37
  647.4 2.8 copy.122
  650.2 2.9 reshape_reshape_transpose_reshape.6
  653.1 4.1 fusion.20
  (237 shorter events, 52.9 us)
Async XLA Ops:
  7.2 352.9 %copy-start = (bf16[1,448,1024]{2,1,0:T(8,128)(2,1)S(1)}, bf16[1,448,1024]{2,1,0:T(8,128)(2,1)}, u32[]{:S(2)}) copy-start(bf16[1,448,1024]{2,1,0:T(8,128)(2,1)} %param.16) | copy-start | bytes 2752516
  7.2 7.8 %copy-start.2 = (bf16[1,128,7168]{2,1,0:T(8,128)(2,1)S(1)}, bf16[1,128,7168]{2,1,0:T(8,128)(2,1)}, u32[]{:S(2)}) copy-start(bf16[1,128,7168]{2,1,0:T(8,128)(2,1)} %param.18) | copy-start | bytes 5505028
  7.2 7.2 %copy-start.6 = (s32[1,128,8]{1,2,0:T(8,128)S(1)}, s32[1,128,8]{1,2,0:T(8,128)}, u32[]{:S(2)}) copy-start(s32[1,128,8]{1,2,0:T(8,128)} %param.19) | copy-start | bytes 12292
  7.2 7.3 %copy-start.7 = (f32[1,128,8]{1,2,0:T(8,128)S(1)}, f32[1,128,8]{1,2,0:T(8,128)}, u32[]{:S(2)}) copy-start(f32[1,128,8]{1,2,0:T(8,128)} %param.20) | copy-start | bytes 12292
  7.2 233.1 %all-gather.2.cloned.1.call-start = ((), (), s32[]{:S(2)}) async-start(), calls=%async_computation.4 | async-start | bytes 15597568 | tf_op jit(solution)/shard_map/all_gather | solution.py:143
  19.3 18.5 %copy-start.5 = (bf16[1,128,1024]{2,1,0:T(8,128)(2,1)S(1)}, bf16[1,128,1024]{2,1,0:T(8,128)(2,1)}, u32[]{:S(2)}) copy-start(bf16[1,128,1024]{2,1,0:T(8,128)(2,1)} %param.13) | copy-start | bytes 786436
  21.1 17.0 %copy-start.8 = (s32[1,16]{1,0:T(1,128)S(1)}, s32[1,16]{1,0:T(1,128)}, u32[]{:S(2)}) copy-start(s32[1,16]{1,0:T(1,128)} %param.21) | copy-start | bytes 196
  21.1 235.5 %all-to-all-start.2 = ((bf16[256,1,1,4,448]{4,3,2,1,0:T(4,128)(2,1)}), bf16[256,1,1,4,448]{4,3,2,1,0:T(4,128)(2,1)}, u32[]{:S(2)}, u32[]{:S(2)}) async-start(bf16[256,1,1,4,448]{4,3,2,1,0:T(4,128)(2,1)} %copy.110), calls=%async_computation.2 | async-start | bytes 2097152 | tf_op jit(solution)/shard_map/all_to_all | solution.py:37
  38.9 6.4 collective-permute-start
  46.0 7.3 %collective-permute-start = (bf16[128,512]{1,0:T(8,128)(2,1)S(1)}, bf16[128,512]{1,0:T(8,128)(2,1)S(1)}, u32[]{:S(2)}, u32[]{:S(2)}) collective-permute-start(bf16[128,512]{1,0:T(8,128)(2,1)S(1)} %get-tuple-element.483), channel_id=1, source_target_pairs={{0,16},{16,32},{32,48},{48,64},{64,80},{80,96},{96,112},{112,128},... | collective-permute-start | bytes 393224 | tf_op jit(solution)/shard_map/while/body/eval_jaxpr/ppermute | solution.py:16
  53.9 9.0 %collective-permute-start = (bf16[128,512]{1,0:T(8,128)(2,1)S(1)}, bf16[128,512]{1,0:T(8,128)(2,1)S(1)}, u32[]{:S(2)}, u32[]{:S(2)}) collective-permute-start(bf16[128,512]{1,0:T(8,128)(2,1)S(1)} %get-tuple-element.483), channel_id=1, source_target_pairs={{0,16},{16,32},{32,48},{48,64},{64,80},{80,96},{96,112},{112,128},... | collective-permute-start | bytes 393224 | tf_op jit(solution)/shard_map/while/body/eval_jaxpr/ppermute | solution.py:16
  63.6 8.3 %collective-permute-start = (bf16[128,512]{1,0:T(8,128)(2,1)S(1)}, bf16[128,512]{1,0:T(8,128)(2,1)S(1)}, u32[]{:S(2)}, u32[]{:S(2)}) collective-permute-start(bf16[128,512]{1,0:T(8,128)(2,1)S(1)} %get-tuple-element.483), channel_id=1, source_target_pairs={{0,16},{16,32},{32,48},{48,64},{64,80},{80,96},{96,112},{112,128},... | collective-permute-start | bytes 393224 | tf_op jit(solution)/shard_map/while/body/eval_jaxpr/ppermute | solution.py:16
  72.5 6.4 collective-permute-start
  79.6 6.3 collective-permute-start
  86.6 15.2 %collective-permute-start = (bf16[128,512]{1,0:T(8,128)(2,1)S(1)}, bf16[128,512]{1,0:T(8,128)(2,1)S(1)}, u32[]{:S(2)}, u32[]{:S(2)}) collective-permute-start(bf16[128,512]{1,0:T(8,128)(2,1)S(1)} %get-tuple-element.483), channel_id=1, source_target_pairs={{0,16},{16,32},{32,48},{48,64},{64,80},{80,96},{96,112},{112,128},... | collective-permute-start | bytes 393224 | tf_op jit(solution)/shard_map/while/body/eval_jaxpr/ppermute | solution.py:16
  102.5 12.9 %collective-permute-start = (bf16[128,512]{1,0:T(8,128)(2,1)S(1)}, bf16[128,512]{1,0:T(8,128)(2,1)S(1)}, u32[]{:S(2)}, u32[]{:S(2)}) collective-permute-start(bf16[128,512]{1,0:T(8,128)(2,1)S(1)} %get-tuple-element.483), channel_id=1, source_target_pairs={{0,16},{16,32},{32,48},{48,64},{64,80},{80,96},{96,112},{112,128},... | collective-permute-start | bytes 393224 | tf_op jit(solution)/shard_map/while/body/eval_jaxpr/ppermute | solution.py:16
  116.1 14.7 %collective-permute-start = (bf16[128,512]{1,0:T(8,128)(2,1)S(1)}, bf16[128,512]{1,0:T(8,128)(2,1)S(1)}, u32[]{:S(2)}, u32[]{:S(2)}) collective-permute-start(bf16[128,512]{1,0:T(8,128)(2,1)S(1)} %get-tuple-element.483), channel_id=1, source_target_pairs={{0,16},{16,32},{32,48},{48,64},{64,80},{80,96},{96,112},{112,128},... | collective-permute-start | bytes 393224 | tf_op jit(solution)/shard_map/while/body/eval_jaxpr/ppermute | solution.py:16
  131.4 18.7 %collective-permute-start = (bf16[128,512]{1,0:T(8,128)(2,1)S(1)}, bf16[128,512]{1,0:T(8,128)(2,1)S(1)}, u32[]{:S(2)}, u32[]{:S(2)}) collective-permute-start(bf16[128,512]{1,0:T(8,128)(2,1)S(1)} %get-tuple-element.483), channel_id=1, source_target_pairs={{0,16},{16,32},{32,48},{48,64},{64,80},{80,96},{96,112},{112,128},... | collective-permute-start | bytes 393224 | tf_op jit(solution)/shard_map/while/body/eval_jaxpr/ppermute | solution.py:16
  150.8 20.1 %collective-permute-start = (bf16[128,512]{1,0:T(8,128)(2,1)S(1)}, bf16[128,512]{1,0:T(8,128)(2,1)S(1)}, u32[]{:S(2)}, u32[]{:S(2)}) collective-permute-start(bf16[128,512]{1,0:T(8,128)(2,1)S(1)} %get-tuple-element.483), channel_id=1, source_target_pairs={{0,16},{16,32},{32,48},{48,64},{64,80},{80,96},{96,112},{112,128},... | collective-permute-start | bytes 393224 | tf_op jit(solution)/shard_map/while/body/eval_jaxpr/ppermute | solution.py:16
  171.6 31.1 %collective-permute-start = (bf16[128,512]{1,0:T(8,128)(2,1)S(1)}, bf16[128,512]{1,0:T(8,128)(2,1)S(1)}, u32[]{:S(2)}, u32[]{:S(2)}) collective-permute-start(bf16[128,512]{1,0:T(8,128)(2,1)S(1)} %get-tuple-element.483), channel_id=1, source_target_pairs={{0,16},{16,32},{32,48},{48,64},{64,80},{80,96},{96,112},{112,128},... | collective-permute-start | bytes 393224 | tf_op jit(solution)/shard_map/while/body/eval_jaxpr/ppermute | solution.py:16
  203.3 10.0 %collective-permute-start = (bf16[128,512]{1,0:T(8,128)(2,1)S(1)}, bf16[128,512]{1,0:T(8,128)(2,1)S(1)}, u32[]{:S(2)}, u32[]{:S(2)}) collective-permute-start(bf16[128,512]{1,0:T(8,128)(2,1)S(1)} %get-tuple-element.483), channel_id=1, source_target_pairs={{0,16},{16,32},{32,48},{48,64},{64,80},{80,96},{96,112},{112,128},... | collective-permute-start | bytes 393224 | tf_op jit(solution)/shard_map/while/body/eval_jaxpr/ppermute | solution.py:16
  214.0 12.4 %collective-permute-start = (bf16[128,512]{1,0:T(8,128)(2,1)S(1)}, bf16[128,512]{1,0:T(8,128)(2,1)S(1)}, u32[]{:S(2)}, u32[]{:S(2)}) collective-permute-start(bf16[128,512]{1,0:T(8,128)(2,1)S(1)} %get-tuple-element.483), channel_id=1, source_target_pairs={{0,16},{16,32},{32,48},{48,64},{64,80},{80,96},{96,112},{112,128},... | collective-permute-start | bytes 393224 | tf_op jit(solution)/shard_map/while/body/eval_jaxpr/ppermute | solution.py:16
  227.1 12.3 %collective-permute-start = (bf16[128,512]{1,0:T(8,128)(2,1)S(1)}, bf16[128,512]{1,0:T(8,128)(2,1)S(1)}, u32[]{:S(2)}, u32[]{:S(2)}) collective-permute-start(bf16[128,512]{1,0:T(8,128)(2,1)S(1)} %get-tuple-element.483), channel_id=1, source_target_pairs={{0,16},{16,32},{32,48},{48,64},{64,80},{80,96},{96,112},{112,128},... | collective-permute-start | bytes 393224 | tf_op jit(solution)/shard_map/while/body/eval_jaxpr/ppermute | solution.py:16
  256.6 101.1 %all-to-all-start = ((bf16[256,1,1,4,448]{4,3,2,1,0:T(4,128)(2,1)}), bf16[256,1,1,4,448]{4,3,2,1,0:T(4,128)(2,1)}, u32[]{:S(2)}, u32[]{:S(2)}) async-start(bf16[256,1,1,4,448]{4,3,2,1,0:T(4,128)(2,1)} %copy.105), calls=%async_computation | async-start | bytes 2097152 | tf_op jit(solution)/shard_map/all_to_all | solution.py:37
  326.6 225.0 %all-reduce.3.cloned.1.call-start = ((), (), s32[]{:S(2)}) async-start(), calls=%async_computation.5 | async-start | bytes 8388608 | tf_op jit(solution)/shard_map/psum | solution.py:172
  555.5 1.3 copy-start.1
  563.3 45.1 %all-to-all-start.3 = ((bf16[256,1,1,4,448]{4,3,2,1,0:T(4,128)(2,1)}), bf16[256,1,1,4,448]{4,3,2,1,0:T(4,128)(2,1)}, u32[]{:S(2)}, u32[]{:S(2)}) async-start(bf16[256,1,1,4,448]{4,3,2,1,0:T(4,128)(2,1)} %bitcast.131), calls=%async_computation.3 | async-start | bytes 2097152 | tf_op jit(solution)/shard_map/all_to_all | solution.py:37
  608.4 39.0 %all-to-all-start.1 = ((bf16[256,1,1,4,448]{4,3,2,1,0:T(4,128)(2,1)}), bf16[256,1,1,4,448]{4,3,2,1,0:T(4,128)(2,1)}, u32[]{:S(2)}, u32[]{:S(2)}) async-start(bf16[256,1,1,4,448]{4,3,2,1,0:T(4,128)(2,1)} %bitcast.130), calls=%async_computation.1 | async-start | bytes 2097152 | tf_op jit(solution)/shard_map/all_to_all | solution.py:37
  616.2 4.1 copy-start.3
  616.2 4.1 copy-start.4
Sparse Core Ops, SparseCore 0:
  10.7 179.2 all-gather.1
  364.0 187.4 all-reduce.2
where the time goes:
time: 665 us; the launch traced here: 664 us
  waiting for transfers between devices  280 us (42%)
  starting transfers between devices  264 us (40%)
  matrix products  49.4 us (7%)
  local copies, waits for them, and re-layouts  40.9 us (6%)
  between operations  14.3 us (2%)
  other arithmetic  13.6 us (2%)
    psum x1, waiting for transfers between devices, sum_all(): return lax.psum(term_rows.astype(jnp.bfloat16), 'ctx').astype(jnp.float32)  188 us
    ppermute x15, starting transfers between devices, shifted(): return lax.ppermute(shard, axis, pairs)  156 us
    all_to_all x4, starting transfers between devices, joined_exchange(): lax.all_to_all(pieces, axis, split_axis=0, concat_axis=0, tiled=True)  108 us
    all_to_all x4, waiting for transfers between devices, joined_exchange(): lax.all_to_all(pieces, axis, split_axis=0, concat_axis=0, tiled=True)  61 us
    ppermute x15, waiting for transfers between devices, shifted(): return lax.ppermute(shard, axis, pairs)  31.3 us
  transfers between devices with their start and end apart: 21, of which 19 were waited for; matrix products, arithmetic and copies ran while one was open for 11% of the time, Pallas kernels for 0%

commit v1 on v0

--- a/solution.py
+++ b/solution.py
@@ -169,7 +169,9 @@
     contract_cols = (((1,), (1,)), ((), ()))
 
     def sum_all(term_rows):
-        return lax.psum(term_rows.astype(jnp.bfloat16), "ctx").astype(jnp.float32)
+        return jnp.sum(lax.all_gather(term_rows.astype(jnp.bfloat16), "ctx"), axis=0).astype(
+            jnp.float32
+        )
 
     pre_full = sum_all(jnp.dot(in_rows, up_part, preferred_element_type=jnp.float32))
     activated = jax.nn.silu(pre_full).astype(jnp.bfloat16)

time: 665 us -> 1070 us (1.61)
  waiting for transfers between devices: 280 us -> 599 us
  blocking collectives: 0 us -> 173 us
  starting transfers between devices: 264 us -> 149 us
  other arithmetic: 13.6 us -> 41.2 us
    all_gather x0 -> x2, waiting for transfers between devices: none -> 545 us  [sum_all(): lax.all_gather(term_rows.astype(jnp.bfloat16), 'ctx')]
    psum x1 -> x0, waiting for transfers between devices: 188 us -> none  [sum_all(): return lax.psum(term_rows.astype(jnp.bfloat16), 'ctx').astype(jnp.float32)]
    all_to_all x0 -> x2, blocking collectives: none -> 173 us  [joined_exchange(): lax.all_to_all(pieces, axis, split_axis=0, concat_axis=0, tiled=True)]
    all_to_all x4 -> x2, starting transfers between devices: 108 us -> 13.9 us  [joined_exchange(): lax.all_to_all(pieces, axis, split_axis=0, concat_axis=0, tiled=True)]
    all_to_all x4 -> x2, waiting for transfers between devices: 61 us -> 18.8 us  [joined_exchange(): lax.all_to_all(pieces, axis, split_axis=0, concat_axis=0, tiled=True)]
    reduce_sum x0 -> x2, other arithmetic: none -> 27.5 us  [sum_all(): jnp.sum(lax.all_gather(term_rows.astype(jnp.bfloat16), 'ctx'), axis=0)]
    ppermute x15, starting transfers between devices: 156 us -> 135 us  [shifted(): return lax.ppermute(shard, axis, pairs)]
  transfers between devices with their start and end apart: 21 -> 20, of which waited for: 19 -> 18; matrix products, arithmetic and copies ran while one was open for 11% -> 9% of each run, Pallas kernels for 0% -> 0%
where the time goes in v1:
time: 1070 us
  waiting for transfers between devices  599 us (56%)
  blocking collectives  173 us (16%)
  starting transfers between devices  149 us (14%)
  matrix products  48.4 us (5%)
  other arithmetic  41.2 us (4%)
  local copies, waits for them, and re-layouts  39.5 us (4%)
  between operations  14.1 us (1%)
    all_gather x2, waiting for transfers between devices, sum_all(): lax.all_gather(term_rows.astype(jnp.bfloat16), 'ctx')  545 us
    all_to_all x2, blocking collectives, joined_exchange(): lax.all_to_all(pieces, axis, split_axis=0, concat_axis=0, tiled=True)  173 us
    ppermute x15, starting transfers between devices, shifted(): return lax.ppermute(shard, axis, pairs)  135 us
    ppermute x15, waiting for transfers between devices, shifted(): return lax.ppermute(shard, axis, pairs)  35 us
    reduce_sum x2, other arithmetic, sum_all(): jnp.sum(lax.all_gather(term_rows.astype(jnp.bfloat16), 'ctx'), axis=0)  27.5 us
  transfers between devices with their start and end apart: 20, of which 18 were waited for; matrix products, arithmetic and copies ran while one was open for 9% of the time, Pallas kernels for 0%

profile of v1, /device:TPU:1, one launch (start us, length us, event | category | flops | bytes accessed | tf_op | source)
XLA Modules:
  0.0 1065.5 jit_solution(6372221204017196223)
XLA Ops:
  9.3 4.5 reduce-window.6
  15.6 183.9 %while.22 = (s32[]{:T(128)}, bf16[128,512]{1,0:T(8,128)(2,1)S(1)}, f32[128,2]{0,1:T(2,128)S(1)}, f32[128,2]{0,1:T(2,128)S(1)}, f32[128,2,512]{2,0,1:T(8,128)S(1)...) while((s32[]{:T(128)}, bf16[128,512]{1,0:T(8,128)(2,1)S(1)}, ...), condition=%wide.region_7.8_spmd.clone, body=%wide.region_3.7_spmd.clone.sunk | while | flops 67740288 | bytes 2839315 | solution.py:133
  15.6 4.6 collective-permute-start
  22.8 4.4 collective-permute-start
  27.4 3.1 collective-permute-done
  31.2 4.4 collective-permute-start
  38.2 4.4 collective-permute-start
  42.8 2.3 collective-permute-done
  45.7 4.4 collective-permute-start
  52.7 4.4 collective-permute-start
  57.3 3.9 collective-permute-done
  61.9 4.4 collective-permute-start
  68.9 4.4 collective-permute-start
  73.5 4.6 collective-permute-done
  78.8 9.7 collective-permute-start
  91.1 9.8 collective-permute-start
  103.5 13.8 %collective-permute-start = (bf16[128,512]{1,0:T(8,128)(2,1)S(1)}, bf16[128,512]{1,0:T(8,128)(2,1)S(1)}, u32[]{:S(2)}, u32[]{:S(2)}) collective-permute-start(bf16[128,512]{1,0:T(8,128)(2,1)S(1)} %get-tuple-element.481), channel_id=1, source_target_pairs={{0,16},{16,32},{32,48},{48,64},{64,80},{80,96},{96,112},{112,128},... | collective-permute-start | bytes 393224 | tf_op jit(solution)/shard_map/while/body/eval_jaxpr/ppermute | solution.py:16
  119.9 18.8 %collective-permute-start = (bf16[128,512]{1,0:T(8,128)(2,1)S(1)}, bf16[128,512]{1,0:T(8,128)(2,1)S(1)}, u32[]{:S(2)}, u32[]{:S(2)}) collective-permute-start(bf16[128,512]{1,0:T(8,128)(2,1)S(1)} %get-tuple-element.481), channel_id=1, source_target_pairs={{0,16},{16,32},{32,48},{48,64},{64,80},{80,96},{96,112},{112,128},... | collective-permute-start | bytes 393224 | tf_op jit(solution)/shard_map/while/body/eval_jaxpr/ppermute | solution.py:16
  141.3 17.1 %collective-permute-start = (bf16[128,512]{1,0:T(8,128)(2,1)S(1)}, bf16[128,512]{1,0:T(8,128)(2,1)S(1)}, u32[]{:S(2)}, u32[]{:S(2)}) collective-permute-start(bf16[128,512]{1,0:T(8,128)(2,1)S(1)} %get-tuple-element.481), channel_id=1, source_target_pairs={{0,16},{16,32},{32,48},{48,64},{64,80},{80,96},{96,112},{112,128},... | collective-permute-start | bytes 393224 | tf_op jit(solution)/shard_map/while/body/eval_jaxpr/ppermute | solution.py:16
  158.7 4.3 collective-permute-done
  163.7 22.9 %collective-permute-start = (bf16[128,512]{1,0:T(8,128)(2,1)S(1)}, bf16[128,512]{1,0:T(8,128)(2,1)S(1)}, u32[]{:S(2)}, u32[]{:S(2)}) collective-permute-start(bf16[128,512]{1,0:T(8,128)(2,1)S(1)} %get-tuple-element.481), channel_id=1, source_target_pairs={{0,16},{16,32},{32,48},{48,64},{64,80},{80,96},{96,112},{112,128},... | collective-permute-start | bytes 393224 | tf_op jit(solution)/shard_map/while/body/eval_jaxpr/ppermute | solution.py:16
  189.2 7.7 collective-permute-start
  200.4 8.3 fusion.16
  210.0 3.1 reshape_reshape.12
  215.7 109.9 %all_to_all.20 = bf16[256,1,1,4,448]{4,3,2,1,0:T(4,128)(2,1)} all-to-all(bf16[256,1,1,4,448]{4,3,2,1,0:T(4,128)(2,1)S(1)} %copy.105), channel_id=1, replica_groups=mesh['ctx'=16,'exp'=16] {'ctx','exp'}, dimensions={0} | all-to-all | bytes 1835008 | tf_op jit(solution)/shard_map/all_to_all | solution.py:37
  325.6 2.4 reshape_reshape.13
  328.0 4.1 convolution_convert_fusion.2
  332.3 2.8 fusion.21
  335.1 3.1 reshape_reshape.14
  341.0 63.4 %all_to_all.21 = bf16[256,1,1,4,448]{4,3,2,1,0:T(4,128)(2,1)} all-to-all(bf16[256,1,1,4,448]{4,3,2,1,0:T(4,128)(2,1)S(1)} %copy.110), channel_id=1, replica_groups=mesh['ctx'=16,'exp'=16] {'ctx','exp'}, dimensions={0} | all-to-all | bytes 1835008 | tf_op jit(solution)/shard_map/all_to_all | solution.py:37
  404.4 2.4 reshape_reshape.15
  406.8 3.8 convolution_convert_fusion.1
  410.6 246.5 %all-gather.8.cloned.1.call-done = bf16[16384,1024]{1,0:T(8,128)(2,1)} async-done(((bf16[1024,1024]{1,0:T(8,128)(2,1)}), bf16[16384,1024]{1,0:T(8,128)(2,1)}) %all-gather.8.cloned.1.call-update) | async-done | bytes 33554448 | tf_op jit(solution)/shard_map/all_gather | solution.py:172
  657.1 14.4 %reduce_sum.119 = bf16[1024,1024]{1,0:T(8,128)(2,1)} reduce(bf16[16,1024,1024]{2,1,0:T(8,128)(2,1)} %bitcast.132, bf16[]{:T(256)} %constant.150.clone.1), dimensions={0}, to_apply=%region_13.14 | reduce | flops 15728640 | bytes 35651584 | tf_op jit(solution)/shard_map/reduce_sum | solution.py:172
  671.5 4.0 convolution_convert_fusion.6
  680.0 6.8 all-to-all-start.1
  686.8 298.4 %all-gather.10.cloned.1.call-done = bf16[16384,1024]{1,0:T(8,128)(2,1)} async-done(((bf16[1024,1024]{1,0:T(8,128)(2,1)}), bf16[16384,1024]{1,0:T(8,128)(2,1)}) %all-gather.10.cloned.1.call-update) | async-done | bytes 33554448 | tf_op jit(solution)/shard_map/all_gather | solution.py:172
  985.2 13.1 %reduce_sum.121 = bf16[1024,1024]{1,0:T(8,128)(2,1)} reduce(bf16[16,1024,1024]{2,1,0:T(8,128)(2,1)} %bitcast.133, bf16[]{:T(256)} %constant.150.clone.1), dimensions={0}, to_apply=%region_15.16 | reduce | flops 15728640 | bytes 35651584 | tf_op jit(solution)/shard_map/reduce_sum | solution.py:172
  998.3 4.0 fusion.29
  1008.3 7.1 all-to-all-start.3
  1015.4 4.1 fusion.31
  1019.5 2.5 fusion.32
  1022.0 2.8 copy.122
  1024.8 2.9 reshape_reshape_transpose_reshape.6
  1027.7 18.8 %all-to-all-done.3 = bf16[256,1,1,4,448]{4,3,2,1,0:T(4,128)(2,1)} async-done(((bf16[256,1,1,4,448]{4,3,2,1,0:T(4,128)(2,1)}), bf16[256,1,1,4,448]{4,3,2,1,0:T(4,128)(2,1)}, u32[]{:S(2)}, u32[]{:S(2)}) %all-to-all-start.3) | async-done | bytes 917536 | tf_op jit(solution)/shard_map/all_to_all | solution.py:37
  1046.5 2.8 copy.121
  1051.5 4.5 fusion.19
  1056.0 3.0 fusion.20
  (244 shorter events, 53.7 us)
Async XLA Ops:
  7.2 399.6 %copy-start = (bf16[1,1024,448]{1,2,0:T(8,128)(2,1)S(1)}, bf16[1,1024,448]{1,2,0:T(8,128)(2,1)}, u32[]{:S(2)}) copy-start(bf16[1,1024,448]{1,2,0:T(8,128)(2,1)} %param.17) | copy-start | bytes 2752516
  7.2 7.2 copy-start.6
  7.2 7.6 copy-start.10
  7.2 193.2 %all-gather.6.cloned.1.call-start = ((), (), s32[]{:S(2)}) async-start(), calls=%async_computation.4 | async-start | bytes 15597568 | tf_op jit(solution)/shard_map/all_gather | solution.py:143
  8.3 648.9 %all-gather.8.cloned.1.call-start = ((), (), s32[]{:S(2)}) async-start(), calls=%async_computation.5 | async-start | bytes 35651584 | tf_op jit(solution)/shard_map/all_gather | solution.py:172
  15.5 184.1 %copy-start.7 = (s32[1,128,8]{1,2,0:T(8,128)S(1)}, s32[1,128,8]{1,2,0:T(8,128)}, u32[]{:S(2)}) copy-start(s32[1,128,8]{1,2,0:T(8,128)} %param.19) | copy-start | bytes 12292
  15.6 184.2 %copy-start.8 = (f32[1,128,8]{1,2,0:T(8,128)S(1)}, f32[1,128,8]{1,2,0:T(8,128)}, u32[]{:S(2)}) copy-start(f32[1,128,8]{1,2,0:T(8,128)} %param.20) | copy-start | bytes 12292
  15.6 6.5 collective-permute-start
  22.8 7.7 collective-permute-start
  31.2 6.3 collective-permute-start
  38.2 6.9 collective-permute-start
  45.7 6.3 collective-permute-start
  52.7 8.5 collective-permute-start
  61.9 6.3 collective-permute-start
  68.9 9.2 collective-permute-start
  78.8 11.6 %collective-permute-start = (bf16[128,512]{1,0:T(8,128)(2,1)S(1)}, bf16[128,512]{1,0:T(8,128)(2,1)S(1)}, u32[]{:S(2)}, u32[]{:S(2)}) collective-permute-start(bf16[128,512]{1,0:T(8,128)(2,1)S(1)} %get-tuple-element.481), channel_id=1, source_target_pairs={{0,16},{16,32},{32,48},{48,64},{64,80},{80,96},{96,112},{112,128},... | collective-permute-start | bytes 393224 | tf_op jit(solution)/shard_map/while/body/eval_jaxpr/ppermute | solution.py:16
  91.1 11.7 %collective-permute-start = (bf16[128,512]{1,0:T(8,128)(2,1)S(1)}, bf16[128,512]{1,0:T(8,128)(2,1)S(1)}, u32[]{:S(2)}, u32[]{:S(2)}) collective-permute-start(bf16[128,512]{1,0:T(8,128)(2,1)S(1)} %get-tuple-element.481), channel_id=1, source_target_pairs={{0,16},{16,32},{32,48},{48,64},{64,80},{80,96},{96,112},{112,128},... | collective-permute-start | bytes 393224 | tf_op jit(solution)/shard_map/while/body/eval_jaxpr/ppermute | solution.py:16
  103.5 15.7 %collective-permute-start = (bf16[128,512]{1,0:T(8,128)(2,1)S(1)}, bf16[128,512]{1,0:T(8,128)(2,1)S(1)}, u32[]{:S(2)}, u32[]{:S(2)}) collective-permute-start(bf16[128,512]{1,0:T(8,128)(2,1)S(1)} %get-tuple-element.481), channel_id=1, source_target_pairs={{0,16},{16,32},{32,48},{48,64},{64,80},{80,96},{96,112},{112,128},... | collective-permute-start | bytes 393224 | tf_op jit(solution)/shard_map/while/body/eval_jaxpr/ppermute | solution.py:16
  119.9 20.8 %collective-permute-start = (bf16[128,512]{1,0:T(8,128)(2,1)S(1)}, bf16[128,512]{1,0:T(8,128)(2,1)S(1)}, u32[]{:S(2)}, u32[]{:S(2)}) collective-permute-start(bf16[128,512]{1,0:T(8,128)(2,1)S(1)} %get-tuple-element.481), channel_id=1, source_target_pairs={{0,16},{16,32},{32,48},{48,64},{64,80},{80,96},{96,112},{112,128},... | collective-permute-start | bytes 393224 | tf_op jit(solution)/shard_map/while/body/eval_jaxpr/ppermute | solution.py:16
  141.3 21.6 %collective-permute-start = (bf16[128,512]{1,0:T(8,128)(2,1)S(1)}, bf16[128,512]{1,0:T(8,128)(2,1)S(1)}, u32[]{:S(2)}, u32[]{:S(2)}) collective-permute-start(bf16[128,512]{1,0:T(8,128)(2,1)S(1)} %get-tuple-element.481), channel_id=1, source_target_pairs={{0,16},{16,32},{32,48},{48,64},{64,80},{80,96},{96,112},{112,128},... | collective-permute-start | bytes 393224 | tf_op jit(solution)/shard_map/while/body/eval_jaxpr/ppermute | solution.py:16
  163.7 24.9 %collective-permute-start = (bf16[128,512]{1,0:T(8,128)(2,1)S(1)}, bf16[128,512]{1,0:T(8,128)(2,1)S(1)}, u32[]{:S(2)}, u32[]{:S(2)}) collective-permute-start(bf16[128,512]{1,0:T(8,128)(2,1)S(1)} %get-tuple-element.481), channel_id=1, source_target_pairs={{0,16},{16,32},{32,48},{48,64},{64,80},{80,96},{96,112},{112,128},... | collective-permute-start | bytes 393224 | tf_op jit(solution)/shard_map/while/body/eval_jaxpr/ppermute | solution.py:16
  189.2 9.6 collective-permute-start
  332.1 653.1 %all-gather.10.cloned.1.call-start = ((), (), s32[]{:S(2)}) async-start(), calls=%async_computation.6 | async-start | bytes 35651584 | tf_op jit(solution)/shard_map/all_gather | solution.py:172
  680.0 328.3 %all-to-all-start.1 = ((bf16[256,1,1,4,448]{4,3,2,1,0:T(4,128)(2,1)}), bf16[256,1,1,4,448]{4,3,2,1,0:T(4,128)(2,1)}, u32[]{:S(2)}, u32[]{:S(2)}) async-start(bf16[256,1,1,4,448]{4,3,2,1,0:T(4,128)(2,1)} %bitcast.135), calls=%async_computation.1 | async-start | bytes 2097152 | tf_op jit(solution)/shard_map/all_to_all | solution.py:37
  998.3 5.4 copy-start.9
  1002.3 1.4 copy-start.3
  1008.3 38.2 %all-to-all-start.3 = ((bf16[256,1,1,4,448]{4,3,2,1,0:T(4,128)(2,1)}), bf16[256,1,1,4,448]{4,3,2,1,0:T(4,128)(2,1)}, u32[]{:S(2)}, u32[]{:S(2)}) async-start(bf16[256,1,1,4,448]{4,3,2,1,0:T(4,128)(2,1)} %bitcast.134), calls=%async_computation.3 | async-start | bytes 2097152 | tf_op jit(solution)/shard_map/all_to_all | solution.py:37
  1015.4 4.1 copy-start.2
  1015.4 4.1 copy-start.5
  1051.5 4.6 copy-start.4
  1056.0 3.0 copy-start.1
Sparse Core Ops, SparseCore 0:
  10.7 162.8 all-gather.5
  332.2 324.9 all-gather.7
  659.9 325.2 all-gather.9
